TPU v7x, 32 devices: a whole 2x2x4 slice. The times are simulated.
32 devices in a mesh: row: 4 (over y, x), col: 8 (over z, core).
Axes of the slice: x: 2, y: 2, z: 4, core: 2. Of those that a mesh axis runs over, the one named last changes fastest.
Arguments:
- features: bfloat16 [16384, 256], P(('col', 'row')), may hold values from -6 to 6
- weight: bfloat16 [256, 256], replicated, may hold values from -0.375 to 0.375
- cotangent: bfloat16 [16384, 256], P(('row', 'col')), may hold values from -6 to 6
- block_index: int32 [4, 8, 32], P('row', 'col'), may hold values from 0 to 511, as said below
- block_count: int32 [4, 8], P('row', 'col'), may hold values from 1 to 32, as said below
- block_values: bfloat16 [4, 8, 32, 128, 128], P('row', 'col'), may hold values from -0.25 to 0.25
Outputs:
- hidden_out: bfloat16 [16384, 256], P(('row', 'col'))
- input_grad: bfloat16 [16384, 256], P(('col', 'row'))
- weight_grad: float32 [256, 256], replicated
Inputs may be any that keep to these rules, and one draw needn't show every extreme that they name: `block_index`: the 32 entries of one tile are distinct; slots at or after the tile's count hold blocks that are not used. `block_count`: at least one tile holds exactly 32 blocks.
All inputs are finite; a program needn't handle non-finite values.
Results may differ from a plain program's by a relative error of at most 0.015.
Values may be sent and summed in bfloat16 or wider, within the bound.
No kernel may reach another device: no remote copies, remote signals or barrier semaphores. Data moves between devices by JAX's collectives and lax.ppermute only.
A program may use at most 64 MiB of HBM per device.

v0:
```python
import math
import jax
import jax.numpy as jnp
from jax import lax
from jax.sharding import PartitionSpec as P

GROUP = 32


def forward_tile(blocks_in, values, index, count, rows_out):
    ncols = blocks_in.shape[0]
    size = blocks_in.shape[1]
    width = blocks_in.shape[2]
    lanes = jnp.arange(GROUP, dtype=jnp.int32)
    targets = jnp.arange(rows_out, dtype=jnp.int32)

    def forward_advance(group_id, totals):
        start = (group_id * GROUP).astype(jnp.int32)
        live = start + lanes < count
        picked = jnp.take(blocks_in, index % ncols, axis=0)
        product = jnp.einsum("gij,gjd->gid", values, picked, preferred_element_type=jnp.float32)
        selector = ((index // ncols)[None, :] == targets[:, None]) & live[None, :]
        return totals + jnp.einsum(
            "rg,gid->rid", selector.astype(jnp.float32), product, precision=lax.Precision.HIGHEST
        )

    zeros = jnp.zeros((rows_out, size, width), jnp.float32)
    groups = (count + GROUP - 1) // GROUP
    return lax.fori_loop(jnp.int32(0), groups, forward_advance, zeros)


def backward_tile(blocks_grad, values, index, count, cols_out):
    size = blocks_grad.shape[1]
    width = blocks_grad.shape[2]
    lanes = jnp.arange(GROUP, dtype=jnp.int32)
    targets = jnp.arange(cols_out, dtype=jnp.int32)

    def backward_advance(group_id, totals):
        start = (group_id * GROUP).astype(jnp.int32)
        live = start + lanes < count
        picked = jnp.take(blocks_grad, index // cols_out, axis=0)
        product = jnp.einsum("gij,gid->gjd", values, picked, preferred_element_type=jnp.float32)
        selector = ((index % cols_out)[None, :] == targets[:, None]) & live[None, :]
        return totals + jnp.einsum(
            "cg,gjd->cjd", selector.astype(jnp.float32), product, precision=lax.Precision.HIGHEST
        )

    zeros = jnp.zeros((cols_out, size, width), jnp.float32)
    groups = (count + GROUP - 1) // GROUP
    return lax.fori_loop(jnp.int32(0), groups, backward_advance, zeros)


def body(features, weight, cotangent, block_index, block_count, block_values):
    row_total = lax.axis_size("row")
    col_total = lax.axis_size("col")
    rows = features.shape[0]
    width = features.shape[1]
    size = block_values.shape[-1]
    block_rows = rows * col_total // size
    block_cols = rows * row_total // size
    index = block_index[0, 0]
    count = block_count[0, 0]
    values = block_values[0, 0]
    gathered = lax.all_gather(features, "row", axis=0, tiled=True)
    projected = jnp.dot(gathered, weight, preferred_element_type=jnp.float32).astype(jnp.bfloat16)
    partial_out = forward_tile(
        projected.reshape(block_cols, size, width), values, index, count, block_rows
    )
    summed_out = lax.psum_scatter(
        partial_out.reshape(block_rows * size, width).astype(jnp.bfloat16),
        "col",
        scatter_dimension=0,
        tiled=True,
    )
    grad_rows = lax.all_gather(cotangent, "col", axis=0, tiled=True)
    partial_back = backward_tile(
        grad_rows.reshape(block_rows, size, width), values, index, count, block_cols
    )
    partial_back = partial_back.reshape(block_cols * size, width)
    grad_sum = lax.psum_scatter(
        partial_back.astype(jnp.bfloat16), "row", scatter_dimension=0, tiled=True
    ).astype(jnp.float32)
    input_grad = jnp.dot(
        grad_sum, weight.astype(jnp.float32).T, precision=lax.Precision.HIGHEST
    ).astype(jnp.bfloat16)
    term = jnp.einsum(
        "nd,ne->de", gathered, partial_back.astype(jnp.bfloat16), preferred_element_type=jnp.float32
    )
    total = lax.psum(term, ("row", "col"))
    nodes = rows * row_total * col_total
    weight_grad = total / math.sqrt(nodes)
    return (summed_out, input_grad, weight_grad)


def solution(mesh):
    in_specs = (
        P(("col", "row"), None),
        P(),
        P(("row", "col"), None),
        P("row", "col", None),
        P("row", "col"),
        P("row", "col", None, None, None),
    )
    out_specs = (P(("row", "col"), None), P(("col", "row"), None), P())
    return jax.shard_map(body, mesh=mesh, in_specs=in_specs, out_specs=out_specs, check_vma=False)
```

profile of v0, /device:TPU:0, one launch (start us, length us, event | category | flops | bytes accessed | tf_op | source)
XLA Modules:
  0.0 277.0 jit_solution(4447913578105518089)
XLA Ops:
  8.0 0.7 all-gather.3.cloned.1.call-update
  11.4 30.1 %all-gather.5.cloned.1.call-done = bf16[4096,256]{1,0:T(8,128)(2,1)} async-done(((bf16[512,256]{1,0:T(8,128)(2,1)}), bf16[4096,256]{1,0:T(8,128)(2,1)}) %all-gather.5.cloned.1.call-update) | async-done | bytes 2097168 | tf_op jit(solution)/shard_map/all_gather | solution.py:75
  41.5 3.6 %gather_fusion.1 = bf16[32,128,256]{2,1,0:T(8,128)(2,1)} fusion(bf16[32,128,256]{2,1,0:T(8,128)(2,1)} %bitcast.94, s32[1024]{0:T(1024)S(1)} %pad_clamp_fusion.1), kind=kCustom, calls=%fused_computation.1 | custom fusion | bytes 4194432 | tf_op jit(solution)/shard_map/while/body/jit(_take)/gather | solution.py:41
  45.8 15.6 %while.34 = (s32[]{:T(128)}, f32[16,128,256]{2,0,1:T(8,128)S(1)}, s32[]{:T(128)}, s32[32]{0:T(128)S(1)}, s32[32]{0:T(128)S(1)}, /*index=5*/s32[]{:T(128)}, s32[3...) while((s32[]{:T(128)}, f32[16,128,256]{2,0,1:T(8,128)S(1)}, ...), condition=%wide.region_4.5_spmd.clone, body=%wide.region_3.4_spmd.clone.sunk | while | flops 471336928 | bytes 24118400 | solution.py:50
  46.5 4.6 %fusion.69 = f32[32,256,128]{2,1,0:T(8,128)} fusion(bf16[32,128,128]{2,1,0:T(8,128)(2,1)} %get-tuple-element.889, bf16[32,128,256]{2,1,0:T(8,128)(2,1)} %get-tuple-element.888, pred[32]{0:T(512)(128)(4,1)S(1)} %get-tuple-element.805), kind=kOutput, calls=%fused_computation.7.clone.1 | convolution fusion | flops 269484032 | bytes 7340064 | tf_op jit(solution)/shard_map/while/body/gij,gid->gjd/dot_general | solution.py:42
  51.1 5.5 %copy.20 = f32[32,256,128]{1,0,2:T(8,128)} copy(f32[32,256,128]{2,1,0:T(8,128)} %fusion.69) | data formatting | bytes 8388608 | tf_op jit(solution)/shard_map/while/body/gij,gid->gjd/dot_general | solution.py:42
  56.6 4.8 %fusion.70 = f32[16,128,256]{2,0,1:T(8,128)S(1)} fusion(f32[16,128,256]{2,0,1:T(8,128)S(1)} %get-tuple-element.871, f32[32,256,128]{1,0,2:T(8,128)} %copy.20, s32[32]{0:T(128)S(1)} %and_select_fusion.6, pred[32]{0:T(512)(128)(4,1)S(1)} %get-tuple-element.806), kind=kOutput, calls=%fused_computation.10.clone.1 | convolution fusion | flops 201851904 | bytes 8388768 | tf_op jit(solution)/shard_map/while/body/cg,gjd->cjd/dot_general | solution.py:44
  61.4 1.1 copy.17
  62.6 6.7 %all-gather.3.cloned.1.call-done = bf16[2048,256]{1,0:T(8,128)(2,1)} async-done(((bf16[512,256]{1,0:T(8,128)(2,1)}), bf16[2048,256]{1,0:T(8,128)(2,1)}) %all-gather.3.cloned.1.call-update) | async-done | bytes 1048592 | tf_op jit(solution)/shard_map/all_gather | solution.py:64
  69.3 2.5 convolution_bitcast_fusion
  72.4 2.5 broadcast_in_dim.62
  74.9 18.6 %while.35 = (s32[]{:T(128)}, f32[32,128,256]{2,0,1:T(8,128)}, s32[]{:T(128)}, s32[1,32]{1,0:T(1,128)S(1)}, s32[32]{0:T(128)S(1)}, /*index=5*/s32[1,32]{1,0:T(1,1...) while((s32[]{:T(128)}, f32[32,128,256]{2,0,1:T(8,128)}, ...), condition=%wide.region_1.2_spmd.clone.clone, body=%wide.region_0.1_spmd.clone.clone.sunk | while | flops 673190272 | bytes 32511760 | solution.py:29
  75.6 0.7 gather_fusion
  76.3 4.0 %fusion.76 = f32[32,256,128]{2,1,0:T(8,128)} fusion(bf16[32,128,128]{2,1,0:T(8,128)(2,1)} %get-tuple-element.856, bf16[32,128,256]{2,1,0:T(8,128)(2,1)S(1)} %gather_fusion, pred[32]{0:T(512)(128)(4,1)S(1)} %get-tuple-element.818), kind=kOutput, calls=%fused_computation.30.clone.1 | convolution fusion | flops 269484032 | bytes 7340064 | tf_op jit(solution)/shard_map/while/body/gij,gjd->gid/dot_general | solution.py:21
  80.3 5.5 %copy.21 = f32[32,256,128]{1,0,2:T(8,128)} copy(f32[32,256,128]{2,1,0:T(8,128)} %fusion.76) | data formatting | bytes 8388608 | tf_op jit(solution)/shard_map/while/body/gij,gjd->gid/dot_general | solution.py:21
  85.8 7.7 %fusion.78 = f32[32,128,256]{2,0,1:T(8,128)} fusion(f32[32,128,256]{2,0,1:T(8,128)} %get-tuple-element.834, f32[32,256,128]{1,0,2:T(8,128)} %copy.21, s32[32]{0:T(128)S(1)} %fusion.77, pred[32]{0:T(512)(128)(4,1)S(1)} %get-tuple-element.819), kind=kOutput, calls=%fused_computation.29.clone.1 | convolution fusion | flops 403703808 | bytes 12583072 | tf_op jit(solution)/shard_map/while/body/rg,gid->rid/dot_general | solution.py:23
  93.5 2.5 convert_element_type.25
  96.0 2.5 copy.11
  98.6 103.3 %all-reduce.2.cloned.1.call-done = f32[256,256]{0,1:T(8,128)} async-done(((f32[256,256]{0,1:T(8,128)}), f32[256,256]{0,1:T(8,128)}) %all-reduce.2.cloned.1.call-update) | async-done | bytes 262160 | tf_op jit(solution)/shard_map/psum | solution.py:89
  201.9 1.0 broadcast_multiply_fusion
  202.9 0.8 copy.13
  203.7 27.9 %reduce-scatter.5.cloned.1.call-done = bf16[512,256]{1,0:T(8,128)(2,1)} async-done(((bf16[2048,256]{1,0:T(8,128)(2,1)}), bf16[512,256]{1,0:T(8,128)(2,1)}) %reduce-scatter.5.cloned.1.call-update) | async-done | bytes 262160 | tf_op jit(solution)/shard_map/reduce_scatter | solution.py:80
  231.7 1.9 convolution_convert_fusion.1
  233.6 36.9 %reduce-scatter.3.cloned.1.call-done = bf16[512,256]{1,0:T(8,128)(2,1)} async-done(((bf16[4096,256]{1,0:T(8,128)(2,1)}), bf16[512,256]{1,0:T(8,128)(2,1)}) %reduce-scatter.3.cloned.1.call-update) | async-done | bytes 262160 | tf_op jit(solution)/shard_map/reduce_scatter | solution.py:69
  (29 shorter events, 5.4 us)
Async XLA Ops:
  7.2 64.7 %copy-start = (bf16[256,256]{1,0:T(8,128)(2,1)S(1)}, bf16[256,256]{1,0:T(8,128)(2,1)}, u32[]{:S(2)}) copy-start(bf16[256,256]{1,0:T(8,128)(2,1)} %param.11) | copy-start | bytes 393220
  7.2 34.3 %all-gather.5.cloned.1.call-start = ((), (), s32[]{:S(2)}) async-start(), calls=%async_computation.4 | async-start | bytes 2359296 | tf_op jit(solution)/shard_map/all_gather | solution.py:75
  7.9 61.3 %all-gather.3.cloned.1.call-start = ((), (), s32[]{:S(2)}) async-start(), calls=%async_computation.2 | async-start | bytes 1310720 | tf_op jit(solution)/shard_map/all_gather | solution.py:64
  8.7 193.3 %all-reduce.2.cloned.1.call-start = ((), (), s32[]{:S(2)}) async-start(), calls=%async_computation.6 | async-start | bytes 524288 | tf_op jit(solution)/shard_map/psum | solution.py:89
  45.1 0.7 copy-start.3
  62.6 9.2 %copy-start.1 = (bf16[16,128,256]{2,1,0:T(8,128)(2,1)}, bf16[16,128,256]{2,1,0:T(8,128)(2,1)S(1)}, u32[]{:S(2)}) copy-start(bf16[16,128,256]{2,1,0:T(8,128)(2,1)S(1)} %copy.17) | copy-start | bytes 3145732
  69.3 2.6 copy-start.2
  71.8 159.9 %reduce-scatter.5.cloned.1.call-start = ((), (), s32[]{:S(2)}) async-start(), calls=%async_computation.5 | async-start | bytes 1310720 | tf_op jit(solution)/shard_map/reduce_scatter | solution.py:80
  72.4 198.1 %reduce-scatter.3.cloned.1.call-start = ((), (), s32[]{:S(2)}) async-start(), calls=%async_computation.3 | async-start | bytes 2359296 | tf_op jit(solution)/shard_map/reduce_scatter | solution.py:69
Sparse Core Ops, SparseCore 0:
  9.6 31.8 all-gather.4
  43.3 25.8 all-gather.2
  75.3 126.5 all-reduce.1
  204.7 26.9 reduce-scatter.4
  234.4 36.0 reduce-scatter.2
where the time goes:
time: 278 us; the launch traced here: 277 us
  waiting for transfers between devices  206 us (74%)
  matrix products  26 us (9%)
  local copies, waits for them, and re-layouts  22.9 us (8%)
  between operations  14.5 us (5%)
  other arithmetic  6.83 us (2%)
    psum x1, waiting for transfers between devices, body(): total = lax.psum(term, ('row', 'col'))  103 us
    reduce_scatter x1, waiting for transfers between devices, body(): lax.psum_scatter(partial_out.reshape(block_rows * size, width).astype(jnp...  36.9 us
    all_gather x1, waiting for transfers between devices, body(): grad_rows = lax.all_gather(cotangent, 'col', axis=0, tiled=True)  30.1 us
    reduce_scatter x1, waiting for transfers between devices, body(): lax.psum_scatter(partial_back.astype(jnp.bfloat16), 'row', scatter_dimens...  27.9 us
    dot_general x1, matrix products, forward_advance(): jnp.einsum('rg,gid->rid', selector.astype(jnp.float32), product, precisio...  7.68 us
    all_gather x1, waiting for transfers between devices, body(): gathered = lax.all_gather(features, 'row', axis=0, tiled=True)  6.68 us
  transfers between devices with their start and end apart: 5, of which 5 were waited for; matrix products, arithmetic and copies ran while one was open for 19% of the time, Pallas kernels for 0%

commit v1 on v0

--- a/solution.py
+++ b/solution.py
@@ -86,7 +86,7 @@
     term = jnp.einsum(
         "nd,ne->de", gathered, partial_back.astype(jnp.bfloat16), preferred_element_type=jnp.float32
     )
-    total = lax.psum(term, ("row", "col"))
+    total = jnp.sum(lax.all_gather(term, ("row", "col")), axis=0)
     nodes = rows * row_total * col_total
     weight_grad = total / math.sqrt(nodes)
     return (summed_out, input_grad, weight_grad)

time: 278 us -> 232 us (0.83)
  waiting for transfers between devices: 206 us -> 150 us
  local copies, waits for them, and re-layouts: 22.9 us -> 32.4 us
    psum x1 -> x0, waiting for transfers between devices: 103 us -> none  [body(): total = lax.psum(term, ('row', 'col'))]
    all_gather x0 -> x1, waiting for transfers between devices: none -> 85.5 us  [body(): total = jnp.sum(lax.all_gather(term, ('row', 'col')), axis=0)]
    reduce_scatter x1, waiting for transfers between devices: 27.9 us -> 1.26 us  [body(): lax.psum_scatter(partial_back.astype(jnp.bfloat16), 'row', scatter_dimens...]
    unnamed x9, local copies, waits for them, and re-layouts: 1.25 us -> 11 us
    reduce_scatter x1, waiting for transfers between devices: 36.9 us -> 27.3 us  [body(): lax.psum_scatter(partial_out.reshape(block_rows * size, width).astype(jnp...]
  transfers between devices with their start and end apart: 5 -> 5, of which waited for: 5 -> 5; matrix products, arithmetic and copies ran while one was open for 19% -> 28% of each run, Pallas kernels for 0% -> 0%
where the time goes in v1:
time: 232 us; the launch traced here: 231 us
  waiting for transfers between devices  150 us (65%)
  local copies, waits for them, and re-layouts  32.4 us (14%)
  matrix products  26.4 us (11%)
  between operations  14.5 us (6%)
  other arithmetic  7.2 us (3%)
    all_gather x1, waiting for transfers between devices, body(): total = jnp.sum(lax.all_gather(term, ('row', 'col')), axis=0)  85.5 us
    all_gather x1, waiting for transfers between devices, body(): grad_rows = lax.all_gather(cotangent, 'col', axis=0, tiled=True)  30.8 us
    reduce_scatter x1, waiting for transfers between devices, body(): lax.psum_scatter(partial_out.reshape(block_rows * size, width).astype(jnp...  27.3 us
    unnamed x9, local copies, waits for them, and re-layouts  11 us
    dot_general x1, matrix products, forward_advance(): jnp.einsum('rg,gid->rid', selector.astype(jnp.float32), product, precisio...  7.76 us
    dot_general x1, local copies, waits for them, and re-layouts, forward_advance(): jnp.einsum('gij,gjd->gid', values, picked, preferred_element_type=jnp.flo...  5.51 us
    dot_general x1, local copies, waits for them, and re-layouts, backward_advance(): jnp.einsum('gij,gid->gjd', values, picked, preferred_element_type=jnp.flo...  5.51 us
    dot_general x1, matrix products, backward_advance(): jnp.einsum('cg,gjd->cjd', selector.astype(jnp.float32), product, precisio...  4.83 us
  transfers between devices with their start and end apart: 5, of which 5 were waited for; matrix products, arithmetic and copies ran while one was open for 28% of the time, Pallas kernels for 0%

profile of v1, /device:TPU:0, one launch (start us, length us, event | category | flops | bytes accessed | tf_op | source)
XLA Modules:
  0.0 231.0 jit_solution(13673392330667548795)
XLA Ops:
  10.7 30.8 %all-gather.7.cloned.1.call-done = bf16[4096,256]{1,0:T(8,128)(2,1)} async-done(((bf16[512,256]{1,0:T(8,128)(2,1)}), bf16[4096,256]{1,0:T(8,128)(2,1)}) %all-gather.7.cloned.1.call-update) | async-done | bytes 2097168 | tf_op jit(solution)/shard_map/all_gather | solution.py:75
  41.5 2.3 gather_fusion.1
  43.8 3.0 %copy.22 = bf16[32,128,256]{1,2,0:T(8,128)(2,1)} copy(bf16[32,128,256]{2,1,0:T(8,128)(2,1)S(1)} %gather_fusion.1) | data formatting | bytes 4194304
  47.4 15.7 %while.34 = (s32[]{:T(128)}, f32[16,128,256]{2,0,1:T(8,128)S(1)}, s32[]{:T(128)}, s32[32]{0:T(128)S(1)}, s32[32]{0:T(128)S(1)}, /*index=5*/s32[]{:T(128)}, s32[3...) while((s32[]{:T(128)}, f32[16,128,256]{2,0,1:T(8,128)S(1)}, ...), condition=%wide.region_4.5_spmd.clone, body=%wide.region_3.4_spmd.clone.sunk | while | flops 471336928 | bytes 24118408 | solution.py:50
  48.1 4.7 %convolution_bitcast_fusion.5 = f32[32,128,256]{1,2,0:T(8,128)} fusion(bf16[32,128,128]{2,1,0:T(8,128)(2,1)} %get-tuple-element.898, bf16[32,128,256]{1,2,0:T(8,128)(2,1)} %get-tuple-element.897, pred[32]{0:T(512)(128)(4,1)S(1)} %get-tuple-element.814), kind=kOutput, calls=%fused_computation.5.clone.1 | convolution fusion | flops 269484032 | bytes 7340064 | tf_op jit(solution)/shard_map/while/body/gij,gid->gjd/dot_general | solution.py:42
  52.7 5.5 %copy.31 = f32[32,128,256]{2,0,1:T(8,128)} copy(f32[32,128,256]{1,2,0:T(8,128)} %convolution_bitcast_fusion.5) | data formatting | bytes 8388608 | tf_op jit(solution)/shard_map/while/body/gij,gid->gjd/dot_general | solution.py:42
  58.3 4.8 %convolution_add_fusion.4 = f32[16,128,256]{2,0,1:T(8,128)S(1)} fusion(f32[16,128,256]{2,0,1:T(8,128)S(1)} %get-tuple-element.880, f32[32,128,256]{2,0,1:T(8,128)} %copy.31, s32[32]{0:T(128)S(1)} %and_select_fusion.6, pred[32]{0:T(512)(128)(4,1)S(1)} %get-tuple-element.815), kind=kOutput, calls=%fused_computation.8.clone.1 | convolution fusion | flops 201851904 | bytes 8388768 | tf_op jit(solution)/shard_map/while/body/cg,gjd->cjd/dot_general | solution.py:44
  63.1 2.1 copy.28
  65.3 4.0 %all-gather.5.cloned.1.call-done = bf16[2048,256]{1,0:T(8,128)(2,1)} async-done(((bf16[512,256]{1,0:T(8,128)(2,1)}), bf16[2048,256]{1,0:T(8,128)(2,1)}) %all-gather.5.cloned.1.call-update) | async-done | bytes 1048592 | tf_op jit(solution)/shard_map/all_gather | solution.py:64
  69.3 2.8 %convolution_bitcast_fusion.2 = f32[256,256]{0,1:T(8,128)} fusion(bf16[2048,256]{1,0:T(8,128)(2,1)} %bitcast.97, bf16[2048,256]{1,0:T(8,128)(2,1)} %all-gather.5.cloned.1.call-done), kind=kOutput, calls=%fused_computation.60 | convolution fusion | flops 268435456 | bytes 2359296 | tf_op jit(solution)/shard_map/nd,ne->de/dot_general | solution.py:86
  72.6 2.5 %broadcast_in_dim.62 = f32[32,128,256]{2,0,1:T(8,128)} broadcast(f32[]{:T(128)} %constant.236.clone.1), dimensions={} | broadcast | bytes 4194308 | tf_op jit(solution)/shard_map/broadcast_in_dim | solution.py:27
  75.1 18.6 %while.35 = (s32[]{:T(128)}, f32[32,128,256]{2,0,1:T(8,128)}, s32[]{:T(128)}, s32[1,32]{1,0:T(1,128)S(1)}, s32[32]{0:T(128)S(1)}, /*index=5*/s32[1,32]{1,0:T(1,1...) while((s32[]{:T(128)}, f32[32,128,256]{2,0,1:T(8,128)}, ...), condition=%wide.region_1.2_spmd.clone.clone, body=%wide.region_0.1_spmd.clone.clone.sunk | while | flops 673190272 | bytes 32511768 | solution.py:29
  76.5 4.0 %convolution_bitcast_fusion.6 = f32[32,128,256]{1,2,0:T(8,128)} fusion(bf16[32,128,128]{2,1,0:T(8,128)(2,1)} %get-tuple-element.865, bf16[32,128,256]{2,1,0:T(8,128)(2,1)S(1)} %gather_fusion, pred[32]{0:T(512)(128)(4,1)S(1)} %get-tuple-element.827), kind=kOutput, calls=%fused_computation.25.clone.1 | convolution fusion | flops 269484032 | bytes 7340064 | tf_op jit(solution)/shard_map/while/body/gij,gjd->gid/dot_general | solution.py:21
  80.5 5.5 %copy.32 = f32[32,128,256]{2,0,1:T(8,128)} copy(f32[32,128,256]{1,2,0:T(8,128)} %convolution_bitcast_fusion.6) | data formatting | bytes 8388608 | tf_op jit(solution)/shard_map/while/body/gij,gjd->gid/dot_general | solution.py:21
  86.0 7.8 %convolution_add_fusion.5 = f32[32,128,256]{2,0,1:T(8,128)} fusion(f32[32,128,256]{2,0,1:T(8,128)} %get-tuple-element.843, f32[32,128,256]{2,0,1:T(8,128)} %copy.32, s32[32]{0:T(128)S(1)} %fusion.60, pred[32]{0:T(512)(128)(4,1)S(1)} %get-tuple-element.828), kind=kOutput, calls=%fused_computation.26.clone.1 | convolution fusion | flops 403703808 | bytes 12583072 | tf_op jit(solution)/shard_map/while/body/rg,gid->rid/dot_general | solution.py:23
  93.8 2.5 %convert_element_type.25 = bf16[32,128,256]{2,0,1:T(8,128)(2,1)S(1)} convert(f32[32,128,256]{2,0,1:T(8,128)} %get-tuple-element.554) | non-fusion elementwise | flops 1048576 | bytes 6291456 | tf_op jit(solution)/shard_map/convert_element_type | solution.py:70
  96.3 2.5 %copy.21 = bf16[32,128,256]{2,1,0:T(8,128)(2,1)} copy(bf16[32,128,256]{2,0,1:T(8,128)(2,1)S(1)} %convert_element_type.25) | data formatting | bytes 4194304 | tf_op jit(solution)/shard_map/convert_element_type | solution.py:70
  98.9 1.3 reduce-scatter.5.cloned.1.call-done
  100.1 1.9 convolution_convert_fusion.1
  102.0 85.5 %all-gather.9.cloned.1.call-done = f32[8192,256]{0,1:T(8,128)} async-done(((f32[256,256]{0,1:T(8,128)}), f32[8192,256]{0,1:T(8,128)}) %all-gather.9.cloned.1.call-update) | async-done | bytes 8388624 | tf_op jit(solution)/shard_map/all_gather | solution.py:89
  187.5 6.8 %copy.26 = f32[32,8,32,256]{3,2,1,0:T(8,128)S(1)} copy(f32[32,8,32,256]{3,1,2,0:T(8,128)} %bitcast.98) | data formatting | bytes 16777216
  194.4 1.9 bitcast_reduce_fusion
  196.4 0.8 copy.24
  197.2 27.3 %reduce-scatter.3.cloned.1.call-done = bf16[512,256]{1,0:T(8,128)(2,1)} async-done(((bf16[4096,256]{1,0:T(8,128)(2,1)}), bf16[512,256]{1,0:T(8,128)(2,1)}) %reduce-scatter.3.cloned.1.call-update) | async-done | bytes 262160 | tf_op jit(solution)/shard_map/reduce_scatter | solution.py:69
  (30 shorter events, 6.1 us)
Async XLA Ops:
  7.2 65.0 %copy-start = (bf16[256,256]{1,0:T(8,128)(2,1)S(1)}, bf16[256,256]{1,0:T(8,128)(2,1)}, u32[]{:S(2)}) copy-start(bf16[256,256]{1,0:T(8,128)(2,1)} %param.11) | copy-start | bytes 393220
  7.2 34.3 %all-gather.7.cloned.1.call-start = ((), (), s32[]{:S(2)}) async-start(), calls=%async_computation.4 | async-start | bytes 2359296 | tf_op jit(solution)/shard_map/all_gather | solution.py:75
  7.9 61.4 %all-gather.5.cloned.1.call-start = ((), (), s32[]{:S(2)}) async-start(), calls=%async_computation.2 | async-start | bytes 1310720 | tf_op jit(solution)/shard_map/all_gather | solution.py:64
  8.7 91.5 %reduce-scatter.5.cloned.1.call-start = ((), (), s32[]{:S(2)}) async-start(), calls=%async_computation.5 | async-start | bytes 1310720 | tf_op jit(solution)/shard_map/reduce_scatter | solution.py:80
  46.7 0.7 copy-start.2
  65.2 122.3 %all-gather.9.cloned.1.call-start = ((), (), s32[]{:S(2)}) async-start(), calls=%async_computation.6 | async-start | bytes 8650752 | tf_op jit(solution)/shard_map/all_gather | solution.py:89
  69.3 2.9 %copy-start.1 = (bf16[2048,256]{1,0:T(8,128)(2,1)S(1)}, bf16[2048,256]{1,0:T(8,128)(2,1)}, u32[]{:S(2)}) copy-start(bf16[2048,256]{1,0:T(8,128)(2,1)} %all-gather.5.cloned.1.call-done) | copy-start | bytes 3145732
  72.1 152.4 %reduce-scatter.3.cloned.1.call-start = ((), (), s32[]{:S(2)}) async-start(), calls=%async_computation.3 | async-start | bytes 2359296 | tf_op jit(solution)/shard_map/reduce_scatter | solution.py:69
Sparse Core Ops, SparseCore 0:
  9.6 31.8 all-gather.6
  43.3 25.8 all-gather.4
  72.2 27.9 reduce-scatter.4
  103.5 84.0 all-gather.8
  190.2 34.2 reduce-scatter.2
